TPU v7x, 32 devices: a whole 2x2x4 slice. The times are simulated.
32 devices in a mesh: prow: 8 (over z, core), pcol: 4 (over y, x).
Axes of the slice: x: 2, y: 2, z: 4, core: 2. Of those that a mesh axis runs over, the one named last changes fastest.
Arguments:
- tri_corners: float32 [9, 2048], P(None, ('prow', 'pcol')), may hold values from -1.6 to 1.6, as said below
- edge_tris: int32 [2, 2048], P(None, 'prow'), may hold values from 0 to 2047, as said below
- edge_free: int32 [2, 2048], P(None, 'prow'), may hold values from 0 to 2
- pivots: int32 [1, 256], replicated, may hold values from 0 to 2047, as said below
- lower_inv: float32 [1, 2, 256, 256], P(None, None, 'prow'), may hold values from -1 to 1, as said below
- upper_inv: float32 [1, 2, 256, 256], P(None, None, 'prow'), may hold values from -2 to 2, as said below
Outputs:
- slab_matrix: float32 [2048, 1024], P('prow', 'pcol')
Inputs may be any that keep to these rules, and one draw needn't show every extreme that they name: `tri_corners`: corners of triangles of area 0.0035 or more. `edge_tris`: the two triangles of edge m differ and both lie in [256 (m // 256), 256 (m // 256) + 256); in each such block every triangle is the plus triangle of exactly one edge. pivots[p, i] is 256 p + i or at least 256 (p + 1); the entries of pivots[p] are distinct. `lower_inv`: each panel's complex matrix is lower triangular with unit diagonal. `upper_inv`: each panel's complex matrix is upper triangular with diagonal entries of modulus 0.5 to 2.
All inputs are finite; a program needn't handle non-finite values.
Results may differ from a plain program's by a relative error of at most 0.0003.
Values sent between devices are 32-bit elements; how exact they have to be, the bound alone decides.
No kernel may reach another device: no remote copies, remote signals or barrier semaphores. Data moves between devices by JAX's collectives and lax.ppermute only.
A program may use at most 64 MiB of HBM per device.

v0:
```python
import math
import jax
import jax.numpy as jnp
from jax import lax
from jax.sharding import PartitionSpec as P

SLAB = 512
PW = 256
wave_number = 2.0 * math.pi
core_square = 0.0025
edge_square = 0.0225
quad_bary = (
    (1.0 / 3.0, 1.0 / 3.0, 1.0 / 3.0),
    (0.05971587178977, 0.470142064105115, 0.470142064105115),
    (0.470142064105115, 0.05971587178977, 0.470142064105115),
    (0.470142064105115, 0.470142064105115, 0.05971587178977),
    (0.797426985353087, 0.101286507323456, 0.101286507323456),
    (0.101286507323456, 0.797426985353087, 0.101286507323456),
    (0.101286507323456, 0.101286507323456, 0.797426985353087),
)
quad_weight = (
    0.225,
    0.132394152788506,
    0.132394152788506,
    0.132394152788506,
    0.125939180544827,
    0.125939180544827,
    0.125939180544827,
)


def broadcast(block, axis, owner):
    block = jnp.where(lax.axis_index(axis) == owner, block, jnp.zeros_like(block))
    return lax.psum(block, axis)


def exact_dot(first_matrix, second_matrix):
    return jnp.dot(first_matrix, second_matrix, precision=lax.Precision.HIGHEST)


def complex_dot(first_real, first_imag, second_real, second_imag):
    out_real = exact_dot(first_real, second_real) - exact_dot(first_imag, second_imag)
    out_imag = exact_dot(first_real, second_imag) + exact_dot(first_imag, second_real)
    return (out_real, out_imag)


def triangle_data(corners, free_index):
    total_count = corners.shape[1]
    vertex = corners.reshape(3, 3, total_count)
    choose = (free_index[None, :] == jnp.arange(3, dtype=jnp.int32)[:, None]).astype(corners.dtype)
    free_vertex = jnp.sum(choose[:, None, :] * vertex, axis=0)
    after_one = jnp.sum(jnp.roll(choose, 1, axis=0)[:, None, :] * vertex, axis=0)
    after_two = jnp.sum(jnp.roll(choose, 2, axis=0)[:, None, :] * vertex, axis=0)
    edge_side = after_one - after_two
    length = jnp.sqrt(jnp.sum(edge_side * edge_side, axis=0))
    normal = jnp.cross(vertex[1] - vertex[0], vertex[2] - vertex[0], axis=0)
    tri_area = 0.5 * jnp.sqrt(jnp.sum(normal * normal, axis=0))
    points = jnp.stack(
        [
            quad_bary[point_index][0] * vertex[0]
            + quad_bary[point_index][1] * vertex[1]
            + quad_bary[point_index][2] * vertex[2]
            for point_index in range(7)
        ],
        axis=1,
    )
    return (points, free_vertex, length, tri_area)


def edge_geometry(plus_corners, minus_corners, plus_free, minus_free):
    plus_points, plus_vertex, length, plus_area = triangle_data(plus_corners, plus_free)
    minus_points, minus_vertex, spare_length, minus_area = triangle_data(minus_corners, minus_free)
    weight = jnp.array(quad_weight, dtype=plus_area.dtype)[:, None]
    plus_vec = (length / (2.0 * plus_area))[None, None, :] * (plus_points - plus_vertex[:, None, :])
    minus_vec = (length / (2.0 * minus_area))[None, None, :] * (
        minus_vertex[:, None, :] - minus_points
    )
    points = jnp.stack([plus_points, minus_points])
    vectors = jnp.stack([plus_vec, minus_vec])
    divergence = jnp.stack([length / plus_area, -length / minus_area])
    weighted = jnp.stack([weight * plus_area[None, :], weight * minus_area[None, :]])
    return (points, vectors, divergence, weighted)


def fill_block(test_geometry, source_geometry):
    test_points, test_vectors, test_div, test_weight = test_geometry
    source_points, source_vectors, source_div, source_weight = source_geometry
    row_count = test_div.shape[1]
    col_count = source_div.shape[1]

    def one_point(point_index, totals):
        real_sum, imag_sum = totals
        for test_sign in range(2):
            here = lax.dynamic_index_in_dim(test_points[test_sign], point_index, 1, keepdims=False)
            along = lax.dynamic_index_in_dim(
                test_vectors[test_sign], point_index, 1, keepdims=False
            )
            test_scale = lax.dynamic_index_in_dim(
                test_weight[test_sign], point_index, 0, keepdims=False
            )
            for source_sign in range(2):
                there = source_points[source_sign]
                other = source_vectors[source_sign]
                gap_x = here[0][None, :, None] - there[0][:, None, :]
                gap_y = here[1][None, :, None] - there[1][:, None, :]
                gap_z = here[2][None, :, None] - there[2][:, None, :]
                distance = jnp.sqrt(gap_x * gap_x + gap_y * gap_y + gap_z * gap_z + core_square)
                inner_product = (
                    along[0][None, :, None] * other[0][:, None, :]
                    + along[1][None, :, None] * other[1][:, None, :]
                    + along[2][None, :, None] * other[2][:, None, :]
                )
                factor = (
                    wave_number * inner_product
                    - test_div[test_sign][None, :, None]
                    * source_div[source_sign][None, None, :]
                    / wave_number
                )
                factor = (
                    factor
                    * (test_scale[None, :, None] * source_weight[source_sign][:, None, :])
                    / (edge_square * distance)
                )
                phase_angle = wave_number * distance
                real_sum = real_sum + jnp.sum(factor * jnp.sin(phase_angle), axis=0)
                imag_sum = imag_sum + jnp.sum(factor * jnp.cos(phase_angle), axis=0)
        return (real_sum, imag_sum)

    empty_sum = jnp.zeros((row_count, col_count), dtype=test_div.dtype)
    return lax.fori_loop(0, 7, one_point, (empty_sum, empty_sum))


def pick_columns(table, local_index):
    table_width = table.shape[1]
    onehot = (jnp.arange(table_width, dtype=jnp.int32)[:, None] == local_index[None, :]).astype(
        jnp.float32
    )
    return exact_dot(table, onehot)


def per_device(tri_corners, edge_tris, edge_free, pivots, lower_inv, upper_inv):
    row_count = edge_tris.shape[1]
    grid_row = lax.axis_index("prow")
    grid_col = lax.axis_index("pcol")
    per_column = SLAB // lax.axis_size("pcol")
    row_block = lax.all_gather(tri_corners, "pcol", axis=1, tiled=True)
    row_base = grid_row * row_count
    test_geometry = edge_geometry(
        pick_columns(row_block, edge_tris[0] - row_base),
        pick_columns(row_block, edge_tris[1] - row_base),
        edge_free[0],
        edge_free[1],
    )
    root_row = grid_col * per_column // row_count
    shared = broadcast(row_block, "prow", root_row)
    tables = broadcast(jnp.concatenate([edge_tris, edge_free], axis=0), "prow", root_row)
    col_base = root_row * row_count
    chosen = lax.dynamic_slice_in_dim(tables, grid_col * per_column - col_base, per_column, 1)
    plus_cols = pick_columns(shared, chosen[0] - col_base)
    minus_cols = pick_columns(shared, chosen[1] - col_base)
    plus_free = chosen[2]
    minus_free = chosen[3]
    source_geometry = edge_geometry(plus_cols, minus_cols, plus_free, minus_free)
    real_part, imag_part = fill_block(test_geometry, source_geometry)
    local_tile = jnp.concatenate([real_part, imag_part], axis=1)
    lower_all, upper_all = (
        lax.all_gather(lower_inv, "prow", axis=2, tiled=True),
        lax.all_gather(upper_inv, "prow", axis=2, tiled=True),
    )
    global_rows = row_base + jnp.arange(row_count, dtype=jnp.int32)
    global_cols = grid_col * per_column + jnp.arange(per_column, dtype=jnp.int32)
    slot_ids = jnp.arange(PW, dtype=jnp.int32)
    finish = PW
    owner_row = 0 // row_count
    pivot_rows = pivots[0]
    select = (pivot_rows[:, None] == global_rows[None, :]).astype(jnp.float32)
    incoming_part = exact_dot(select, local_tile)
    local_start = 0 - owner_row * row_count
    diagonal_part = local_tile[local_start : local_start + PW]
    incoming = lax.psum(incoming_part, "prow")
    initial = broadcast(diagonal_part, "prow", owner_row)
    moved_rows = (
        (global_rows[:, None] == pivot_rows[None, :])
        & (pivot_rows[None, :] != 0 + slot_ids[None, :])
    ).astype(jnp.float32)
    swapped_in = exact_dot(moved_rows, initial)
    was_moved = jnp.sum(moved_rows, axis=1) > 0.5
    on_diagonal = (global_rows[:, None] == 0 + slot_ids[None, :]).astype(jnp.float32)
    from_pivots = exact_dot(on_diagonal, incoming)
    in_block = (global_rows >= 0) & (global_rows < finish)
    local_tile = jnp.where(
        in_block[:, None], from_pivots, jnp.where(was_moved[:, None], swapped_in, local_tile)
    )
    padded = lax.dynamic_update_slice(
        jnp.zeros((2, SLAB, PW), jnp.float32), upper_all[0], (0, 0, 0)
    )
    segment = lax.all_gather(local_tile, "pcol", axis=1, tiled=True)
    shards = segment.shape[1] // (2 * per_column)
    shaped = segment.reshape(row_count, shards, 2, per_column)
    segment_real = shaped[:, :, 0, :].reshape(row_count, shards * per_column)
    segment_imag = shaped[:, :, 1, :].reshape(row_count, shards * per_column)
    weights = lax.dynamic_slice_in_dim(padded, jnp.int32(0) // 2, shards * per_column, 1)
    out_real, out_imag = complex_dot(segment_real, segment_imag, weights[0], weights[1])
    left_factor = jnp.zeros((row_count, 2 * PW), jnp.float32) + jnp.concatenate(
        [out_real, out_imag], axis=1
    )
    lower_now = lower_all[0]
    right_real, right_imag = complex_dot(
        lower_now[0], lower_now[1], incoming[:, :per_column], incoming[:, per_column:]
    )
    left_real = left_factor[:, :PW]
    left_imag = left_factor[:, PW:]
    update_real, update_imag = complex_dot(left_real, left_imag, right_real, right_imag)
    col_offset = jnp.clip(grid_col * per_column - 0, 0, PW - per_column)
    panel_real = lax.dynamic_slice_in_dim(left_real, col_offset, per_column, 1)
    panel_imag = lax.dynamic_slice_in_dim(left_imag, col_offset, per_column, 1)
    below = global_rows >= finish
    trailing = below[:, None] & (global_cols >= finish)[None, :]
    in_panel = below[:, None] & ((global_cols >= 0) & (global_cols < finish))[None, :]
    tile_real = local_tile[:, :per_column]
    tile_imag = local_tile[:, per_column:]
    new_real = jnp.where(
        trailing, tile_real - update_real, jnp.where(in_panel, panel_real, tile_real)
    )
    new_imag = jnp.where(
        trailing, tile_imag - update_imag, jnp.where(in_panel, panel_imag, tile_imag)
    )
    local_tile = jnp.concatenate([new_real, new_imag], axis=1)
    return local_tile


def solution(mesh):
    in_specs = (
        P(None, ("prow", "pcol")),
        P(None, "prow"),
        P(None, "prow"),
        P(),
        P(None, None, "prow", None),
        P(None, None, "prow", None),
    )
    out_specs = P("prow", "pcol")
    return jax.shard_map(
        per_device, mesh=mesh, in_specs=in_specs, out_specs=out_specs, check_vma=False
    )
```

profile of v0, /device:TPU:0, one launch (start us, length us, event | category | flops | bytes accessed | tf_op | source)
XLA Modules:
  0.0 290.3 jit_solution(5166626255349097872)
XLA Ops:
  6.5 0.7 copy-done.8
  7.9 10.7 %psum.28 = s32[4,256]{1,0:T(4,128)S(1)} all-reduce(s32[4,256]{1,0:T(4,128)S(1)} %add_select_fusion), channel_id=1, replica_groups=mesh['prow'=8,'pcol'=4] {'prow'}, use_global_device_ids=true, to_apply=%region_6.8 | all-reduce | flops 1024 | bytes 8192 | tf_op jit(solution)/shard_map/psum | solution.py:34
  19.3 8.2 %all-gather = f32[4,64,9]{1,2,0:T(8,128)S(1)} all-gather(f32[1,64,9]{1,2,0:T(8,128)S(1)} %bitcast.272), channel_id=1, replica_groups=mesh['prow'=8,'pcol'=4] {'pcol'}, dimensions={0}, use_global_device_ids=true | all-gather | bytes 11520 | tf_op jit(solution)/shard_map/all_gather | solution.py:146
  27.9 25.9 %psum.29 = f32[9,256]{1,0:T(8,128)S(1)} all-reduce(f32[9,256]{1,0:T(8,128)S(1)} %select_bitcast_fusion), channel_id=1, replica_groups=mesh['prow'=8,'pcol'=4] {'prow'}, use_global_device_ids=true, to_apply=%region_5.7 | all-reduce | flops 2304 | bytes 18432 | tf_op jit(solution)/shard_map/psum | solution.py:34
  56.0 128.9 %while.18 = (s32[]{:T(128)}, f32[256,128]{1,0:T(8,128)S(1)}, f32[256,128]{1,0:T(8,128)S(1)}, f32[3,7,256]{2,1,0:T(8,128)S(1)}, f32[3,7,128]{2,1,0:T(8,128)S(1)},...) while((s32[]{:T(128)}, f32[256,128]{1,0:T(8,128)S(1)}, ...), condition=%wide.region_25.28_spmd.clone.clone.clone, body=%wide.region_16.27_spmd.clone.clone.clone.sunk | while | flops 23267076 | bytes 3925331 | solution.py:130
  56.4 4.5 %multiply_reduce_fusion.22 = (f32[256,128]{1,0:T(8,128)S(1)}, f32[256,128]{1,0:T(8,128)S(1)}) fusion(f32[256]{0:T(256)S(1)} %bitcast.245, f32[256]{0:T(256)S(1)} %bitcast.243, f32[256]{0:T(256)S(1)} %bitcast.241, f32[7,128]{1,0:T(8,128)S(1)} %get-tuple-element.879, f32[7,128]{1,0:T(8,128)S(1)} %get-tuple-element.880, ...), kind=kLoop, calls=%fused_computation.2.clone.1 | loop fusion | flops 5668864 | bytes 425472 | tf_op jit(solution)/shard_map/while/body/eval_jaxpr/reduce_sum | solution.py:126
  60.8 4.5 %multiply_reduce_fusion.24 = (f32[256,128]{1,0:T(8,128)S(1)}, f32[256,128]{1,0:T(8,128)S(1)}) fusion(f32[7,128]{1,0:T(8,128)S(1)} %get-tuple-element.879, f32[7,128]{1,0:T(8,128)S(1)} %get-tuple-element.880, f32[7,128]{1,0:T(8,128)S(1)} %get-tuple-element.881, f32[256]{0:T(256)S(1)} %bitcast.257, f32[256]{0:T(256)S(1)} %bitcast.255, ...), kind=kLoop, calls=%fused_computation.4.clone.1 | loop fusion | flops 5668864 | bytes 425472 | tf_op jit(solution)/shard_map/while/body/eval_jaxpr/reduce_sum | solution.py:126
  65.3 4.5 %multiply_reduce_fusion.25 = (f32[256,128]{1,0:T(8,128)S(1)}, f32[256,128]{1,0:T(8,128)S(1)}) fusion(f32[7,128]{1,0:T(8,128)S(1)} %get-tuple-element.891, f32[256]{0:T(256)S(1)} %bitcast.258, f32[7,128]{1,0:T(8,128)S(1)} %get-tuple-element.892, f32[256]{0:T(256)S(1)} %bitcast.256, f32[7,128]{1,0:T(8,128)S(1)} %get-tuple-element.893, ...), kind=kLoop, calls=%fused_computation.5.clone.1 | loop fusion | flops 5668864 | bytes 425472 | tf_op jit(solution)/shard_map/while/body/eval_jaxpr/reduce_sum | solution.py:126
  69.8 4.5 %multiply_reduce_fusion.23 = (f32[256,128]{1,0:T(8,128)S(1)}, f32[256,128]{1,0:T(8,128)S(1)}) fusion(f32[256]{0:T(256)S(1)} %bitcast.246, f32[256]{0:T(256)S(1)} %bitcast.244, f32[256]{0:T(256)S(1)} %bitcast.242, f32[7,128]{1,0:T(8,128)S(1)} %get-tuple-element.891, f32[7,128]{1,0:T(8,128)S(1)} %get-tuple-element.892, ...), kind=kLoop, calls=%fused_computation.3.clone.1 | loop fusion | flops 5668864 | bytes 425472 | tf_op jit(solution)/shard_map/while/body/eval_jaxpr/reduce_sum | solution.py:126
  74.8 4.5 %multiply_reduce_fusion.22 = (f32[256,128]{1,0:T(8,128)S(1)}, f32[256,128]{1,0:T(8,128)S(1)}) fusion(f32[256]{0:T(256)S(1)} %bitcast.245, f32[256]{0:T(256)S(1)} %bitcast.243, f32[256]{0:T(256)S(1)} %bitcast.241, f32[7,128]{1,0:T(8,128)S(1)} %get-tuple-element.879, f32[7,128]{1,0:T(8,128)S(1)} %get-tuple-element.880, ...), kind=kLoop, calls=%fused_computation.2.clone.1 | loop fusion | flops 5668864 | bytes 425472 | tf_op jit(solution)/shard_map/while/body/eval_jaxpr/reduce_sum | solution.py:126
  79.3 4.5 %multiply_reduce_fusion.24 = (f32[256,128]{1,0:T(8,128)S(1)}, f32[256,128]{1,0:T(8,128)S(1)}) fusion(f32[7,128]{1,0:T(8,128)S(1)} %get-tuple-element.879, f32[7,128]{1,0:T(8,128)S(1)} %get-tuple-element.880, f32[7,128]{1,0:T(8,128)S(1)} %get-tuple-element.881, f32[256]{0:T(256)S(1)} %bitcast.257, f32[256]{0:T(256)S(1)} %bitcast.255, ...), kind=kLoop, calls=%fused_computation.4.clone.1 | loop fusion | flops 5668864 | bytes 425472 | tf_op jit(solution)/shard_map/while/body/eval_jaxpr/reduce_sum | solution.py:126
  83.7 4.5 %multiply_reduce_fusion.25 = (f32[256,128]{1,0:T(8,128)S(1)}, f32[256,128]{1,0:T(8,128)S(1)}) fusion(f32[7,128]{1,0:T(8,128)S(1)} %get-tuple-element.891, f32[256]{0:T(256)S(1)} %bitcast.258, f32[7,128]{1,0:T(8,128)S(1)} %get-tuple-element.892, f32[256]{0:T(256)S(1)} %bitcast.256, f32[7,128]{1,0:T(8,128)S(1)} %get-tuple-element.893, ...), kind=kLoop, calls=%fused_computation.5.clone.1 | loop fusion | flops 5668864 | bytes 425472 | tf_op jit(solution)/shard_map/while/body/eval_jaxpr/reduce_sum | solution.py:126
  88.2 4.5 %multiply_reduce_fusion.23 = (f32[256,128]{1,0:T(8,128)S(1)}, f32[256,128]{1,0:T(8,128)S(1)}) fusion(f32[256]{0:T(256)S(1)} %bitcast.246, f32[256]{0:T(256)S(1)} %bitcast.244, f32[256]{0:T(256)S(1)} %bitcast.242, f32[7,128]{1,0:T(8,128)S(1)} %get-tuple-element.891, f32[7,128]{1,0:T(8,128)S(1)} %get-tuple-element.892, ...), kind=kLoop, calls=%fused_computation.3.clone.1 | loop fusion | flops 5668864 | bytes 425472 | tf_op jit(solution)/shard_map/while/body/eval_jaxpr/reduce_sum | solution.py:126
  93.2 4.5 %multiply_reduce_fusion.22 = (f32[256,128]{1,0:T(8,128)S(1)}, f32[256,128]{1,0:T(8,128)S(1)}) fusion(f32[256]{0:T(256)S(1)} %bitcast.245, f32[256]{0:T(256)S(1)} %bitcast.243, f32[256]{0:T(256)S(1)} %bitcast.241, f32[7,128]{1,0:T(8,128)S(1)} %get-tuple-element.879, f32[7,128]{1,0:T(8,128)S(1)} %get-tuple-element.880, ...), kind=kLoop, calls=%fused_computation.2.clone.1 | loop fusion | flops 5668864 | bytes 425472 | tf_op jit(solution)/shard_map/while/body/eval_jaxpr/reduce_sum | solution.py:126
  97.7 4.5 %multiply_reduce_fusion.24 = (f32[256,128]{1,0:T(8,128)S(1)}, f32[256,128]{1,0:T(8,128)S(1)}) fusion(f32[7,128]{1,0:T(8,128)S(1)} %get-tuple-element.879, f32[7,128]{1,0:T(8,128)S(1)} %get-tuple-element.880, f32[7,128]{1,0:T(8,128)S(1)} %get-tuple-element.881, f32[256]{0:T(256)S(1)} %bitcast.257, f32[256]{0:T(256)S(1)} %bitcast.255, ...), kind=kLoop, calls=%fused_computation.4.clone.1 | loop fusion | flops 5668864 | bytes 425472 | tf_op jit(solution)/shard_map/while/body/eval_jaxpr/reduce_sum | solution.py:126
  102.2 4.5 %multiply_reduce_fusion.25 = (f32[256,128]{1,0:T(8,128)S(1)}, f32[256,128]{1,0:T(8,128)S(1)}) fusion(f32[7,128]{1,0:T(8,128)S(1)} %get-tuple-element.891, f32[256]{0:T(256)S(1)} %bitcast.258, f32[7,128]{1,0:T(8,128)S(1)} %get-tuple-element.892, f32[256]{0:T(256)S(1)} %bitcast.256, f32[7,128]{1,0:T(8,128)S(1)} %get-tuple-element.893, ...), kind=kLoop, calls=%fused_computation.5.clone.1 | loop fusion | flops 5668864 | bytes 425472 | tf_op jit(solution)/shard_map/while/body/eval_jaxpr/reduce_sum | solution.py:126
  106.6 4.5 %multiply_reduce_fusion.23 = (f32[256,128]{1,0:T(8,128)S(1)}, f32[256,128]{1,0:T(8,128)S(1)}) fusion(f32[256]{0:T(256)S(1)} %bitcast.246, f32[256]{0:T(256)S(1)} %bitcast.244, f32[256]{0:T(256)S(1)} %bitcast.242, f32[7,128]{1,0:T(8,128)S(1)} %get-tuple-element.891, f32[7,128]{1,0:T(8,128)S(1)} %get-tuple-element.892, ...), kind=kLoop, calls=%fused_computation.3.clone.1 | loop fusion | flops 5668864 | bytes 425472 | tf_op jit(solution)/shard_map/while/body/eval_jaxpr/reduce_sum | solution.py:126
  111.6 4.5 %multiply_reduce_fusion.22 = (f32[256,128]{1,0:T(8,128)S(1)}, f32[256,128]{1,0:T(8,128)S(1)}) fusion(f32[256]{0:T(256)S(1)} %bitcast.245, f32[256]{0:T(256)S(1)} %bitcast.243, f32[256]{0:T(256)S(1)} %bitcast.241, f32[7,128]{1,0:T(8,128)S(1)} %get-tuple-element.879, f32[7,128]{1,0:T(8,128)S(1)} %get-tuple-element.880, ...), kind=kLoop, calls=%fused_computation.2.clone.1 | loop fusion | flops 5668864 | bytes 425472 | tf_op jit(solution)/shard_map/while/body/eval_jaxpr/reduce_sum | solution.py:126
  116.1 4.5 %multiply_reduce_fusion.24 = (f32[256,128]{1,0:T(8,128)S(1)}, f32[256,128]{1,0:T(8,128)S(1)}) fusion(f32[7,128]{1,0:T(8,128)S(1)} %get-tuple-element.879, f32[7,128]{1,0:T(8,128)S(1)} %get-tuple-element.880, f32[7,128]{1,0:T(8,128)S(1)} %get-tuple-element.881, f32[256]{0:T(256)S(1)} %bitcast.257, f32[256]{0:T(256)S(1)} %bitcast.255, ...), kind=kLoop, calls=%fused_computation.4.clone.1 | loop fusion | flops 5668864 | bytes 425472 | tf_op jit(solution)/shard_map/while/body/eval_jaxpr/reduce_sum | solution.py:126
  120.6 4.5 %multiply_reduce_fusion.25 = (f32[256,128]{1,0:T(8,128)S(1)}, f32[256,128]{1,0:T(8,128)S(1)}) fusion(f32[7,128]{1,0:T(8,128)S(1)} %get-tuple-element.891, f32[256]{0:T(256)S(1)} %bitcast.258, f32[7,128]{1,0:T(8,128)S(1)} %get-tuple-element.892, f32[256]{0:T(256)S(1)} %bitcast.256, f32[7,128]{1,0:T(8,128)S(1)} %get-tuple-element.893, ...), kind=kLoop, calls=%fused_computation.5.clone.1 | loop fusion | flops 5668864 | bytes 425472 | tf_op jit(solution)/shard_map/while/body/eval_jaxpr/reduce_sum | solution.py:126
  125.1 4.5 %multiply_reduce_fusion.23 = (f32[256,128]{1,0:T(8,128)S(1)}, f32[256,128]{1,0:T(8,128)S(1)}) fusion(f32[256]{0:T(256)S(1)} %bitcast.246, f32[256]{0:T(256)S(1)} %bitcast.244, f32[256]{0:T(256)S(1)} %bitcast.242, f32[7,128]{1,0:T(8,128)S(1)} %get-tuple-element.891, f32[7,128]{1,0:T(8,128)S(1)} %get-tuple-element.892, ...), kind=kLoop, calls=%fused_computation.3.clone.1 | loop fusion | flops 5668864 | bytes 425472 | tf_op jit(solution)/shard_map/while/body/eval_jaxpr/reduce_sum | solution.py:126
  130.1 4.5 %multiply_reduce_fusion.22 = (f32[256,128]{1,0:T(8,128)S(1)}, f32[256,128]{1,0:T(8,128)S(1)}) fusion(f32[256]{0:T(256)S(1)} %bitcast.245, f32[256]{0:T(256)S(1)} %bitcast.243, f32[256]{0:T(256)S(1)} %bitcast.241, f32[7,128]{1,0:T(8,128)S(1)} %get-tuple-element.879, f32[7,128]{1,0:T(8,128)S(1)} %get-tuple-element.880, ...), kind=kLoop, calls=%fused_computation.2.clone.1 | loop fusion | flops 5668864 | bytes 425472 | tf_op jit(solution)/shard_map/while/body/eval_jaxpr/reduce_sum | solution.py:126
  134.5 4.5 %multiply_reduce_fusion.24 = (f32[256,128]{1,0:T(8,128)S(1)}, f32[256,128]{1,0:T(8,128)S(1)}) fusion(f32[7,128]{1,0:T(8,128)S(1)} %get-tuple-element.879, f32[7,128]{1,0:T(8,128)S(1)} %get-tuple-element.880, f32[7,128]{1,0:T(8,128)S(1)} %get-tuple-element.881, f32[256]{0:T(256)S(1)} %bitcast.257, f32[256]{0:T(256)S(1)} %bitcast.255, ...), kind=kLoop, calls=%fused_computation.4.clone.1 | loop fusion | flops 5668864 | bytes 425472 | tf_op jit(solution)/shard_map/while/body/eval_jaxpr/reduce_sum | solution.py:126
  139.0 4.5 %multiply_reduce_fusion.25 = (f32[256,128]{1,0:T(8,128)S(1)}, f32[256,128]{1,0:T(8,128)S(1)}) fusion(f32[7,128]{1,0:T(8,128)S(1)} %get-tuple-element.891, f32[256]{0:T(256)S(1)} %bitcast.258, f32[7,128]{1,0:T(8,128)S(1)} %get-tuple-element.892, f32[256]{0:T(256)S(1)} %bitcast.256, f32[7,128]{1,0:T(8,128)S(1)} %get-tuple-element.893, ...), kind=kLoop, calls=%fused_computation.5.clone.1 | loop fusion | flops 5668864 | bytes 425472 | tf_op jit(solution)/shard_map/while/body/eval_jaxpr/reduce_sum | solution.py:126
  143.5 4.5 %multiply_reduce_fusion.23 = (f32[256,128]{1,0:T(8,128)S(1)}, f32[256,128]{1,0:T(8,128)S(1)}) fusion(f32[256]{0:T(256)S(1)} %bitcast.246, f32[256]{0:T(256)S(1)} %bitcast.244, f32[256]{0:T(256)S(1)} %bitcast.242, f32[7,128]{1,0:T(8,128)S(1)} %get-tuple-element.891, f32[7,128]{1,0:T(8,128)S(1)} %get-tuple-element.892, ...), kind=kLoop, calls=%fused_computation.3.clone.1 | loop fusion | flops 5668864 | bytes 425472 | tf_op jit(solution)/shard_map/while/body/eval_jaxpr/reduce_sum | solution.py:126
  148.5 4.5 %multiply_reduce_fusion.22 = (f32[256,128]{1,0:T(8,128)S(1)}, f32[256,128]{1,0:T(8,128)S(1)}) fusion(f32[256]{0:T(256)S(1)} %bitcast.245, f32[256]{0:T(256)S(1)} %bitcast.243, f32[256]{0:T(256)S(1)} %bitcast.241, f32[7,128]{1,0:T(8,128)S(1)} %get-tuple-element.879, f32[7,128]{1,0:T(8,128)S(1)} %get-tuple-element.880, ...), kind=kLoop, calls=%fused_computation.2.clone.1 | loop fusion | flops 5668864 | bytes 425472 | tf_op jit(solution)/shard_map/while/body/eval_jaxpr/reduce_sum | solution.py:126
  153.0 4.5 %multiply_reduce_fusion.24 = (f32[256,128]{1,0:T(8,128)S(1)}, f32[256,128]{1,0:T(8,128)S(1)}) fusion(f32[7,128]{1,0:T(8,128)S(1)} %get-tuple-element.879, f32[7,128]{1,0:T(8,128)S(1)} %get-tuple-element.880, f32[7,128]{1,0:T(8,128)S(1)} %get-tuple-element.881, f32[256]{0:T(256)S(1)} %bitcast.257, f32[256]{0:T(256)S(1)} %bitcast.255, ...), kind=kLoop, calls=%fused_computation.4.clone.1 | loop fusion | flops 5668864 | bytes 425472 | tf_op jit(solution)/shard_map/while/body/eval_jaxpr/reduce_sum | solution.py:126
  157.4 4.5 %multiply_reduce_fusion.25 = (f32[256,128]{1,0:T(8,128)S(1)}, f32[256,128]{1,0:T(8,128)S(1)}) fusion(f32[7,128]{1,0:T(8,128)S(1)} %get-tuple-element.891, f32[256]{0:T(256)S(1)} %bitcast.258, f32[7,128]{1,0:T(8,128)S(1)} %get-tuple-element.892, f32[256]{0:T(256)S(1)} %bitcast.256, f32[7,128]{1,0:T(8,128)S(1)} %get-tuple-element.893, ...), kind=kLoop, calls=%fused_computation.5.clone.1 | loop fusion | flops 5668864 | bytes 425472 | tf_op jit(solution)/shard_map/while/body/eval_jaxpr/reduce_sum | solution.py:126
  161.9 4.5 %multiply_reduce_fusion.23 = (f32[256,128]{1,0:T(8,128)S(1)}, f32[256,128]{1,0:T(8,128)S(1)}) fusion(f32[256]{0:T(256)S(1)} %bitcast.246, f32[256]{0:T(256)S(1)} %bitcast.244, f32[256]{0:T(256)S(1)} %bitcast.242, f32[7,128]{1,0:T(8,128)S(1)} %get-tuple-element.891, f32[7,128]{1,0:T(8,128)S(1)} %get-tuple-element.892, ...), kind=kLoop, calls=%fused_computation.3.clone.1 | loop fusion | flops 5668864 | bytes 425472 | tf_op jit(solution)/shard_map/while/body/eval_jaxpr/reduce_sum | solution.py:126
  166.9 4.5 %multiply_reduce_fusion.22 = (f32[256,128]{1,0:T(8,128)S(1)}, f32[256,128]{1,0:T(8,128)S(1)}) fusion(f32[256]{0:T(256)S(1)} %bitcast.245, f32[256]{0:T(256)S(1)} %bitcast.243, f32[256]{0:T(256)S(1)} %bitcast.241, f32[7,128]{1,0:T(8,128)S(1)} %get-tuple-element.879, f32[7,128]{1,0:T(8,128)S(1)} %get-tuple-element.880, ...), kind=kLoop, calls=%fused_computation.2.clone.1 | loop fusion | flops 5668864 | bytes 425472 | tf_op jit(solution)/shard_map/while/body/eval_jaxpr/reduce_sum | solution.py:126
  171.4 4.5 %multiply_reduce_fusion.24 = (f32[256,128]{1,0:T(8,128)S(1)}, f32[256,128]{1,0:T(8,128)S(1)}) fusion(f32[7,128]{1,0:T(8,128)S(1)} %get-tuple-element.879, f32[7,128]{1,0:T(8,128)S(1)} %get-tuple-element.880, f32[7,128]{1,0:T(8,128)S(1)} %get-tuple-element.881, f32[256]{0:T(256)S(1)} %bitcast.257, f32[256]{0:T(256)S(1)} %bitcast.255, ...), kind=kLoop, calls=%fused_computation.4.clone.1 | loop fusion | flops 5668864 | bytes 425472 | tf_op jit(solution)/shard_map/while/body/eval_jaxpr/reduce_sum | solution.py:126
  175.9 4.5 %multiply_reduce_fusion.25 = (f32[256,128]{1,0:T(8,128)S(1)}, f32[256,128]{1,0:T(8,128)S(1)}) fusion(f32[7,128]{1,0:T(8,128)S(1)} %get-tuple-element.891, f32[256]{0:T(256)S(1)} %bitcast.258, f32[7,128]{1,0:T(8,128)S(1)} %get-tuple-element.892, f32[256]{0:T(256)S(1)} %bitcast.256, f32[7,128]{1,0:T(8,128)S(1)} %get-tuple-element.893, ...), kind=kLoop, calls=%fused_computation.5.clone.1 | loop fusion | flops 5668864 | bytes 425472 | tf_op jit(solution)/shard_map/while/body/eval_jaxpr/reduce_sum | solution.py:126
  180.3 4.5 %multiply_reduce_fusion.23 = (f32[256,128]{1,0:T(8,128)S(1)}, f32[256,128]{1,0:T(8,128)S(1)}) fusion(f32[256]{0:T(256)S(1)} %bitcast.246, f32[256]{0:T(256)S(1)} %bitcast.244, f32[256]{0:T(256)S(1)} %bitcast.242, f32[7,128]{1,0:T(8,128)S(1)} %get-tuple-element.891, f32[7,128]{1,0:T(8,128)S(1)} %get-tuple-element.892, ...), kind=kLoop, calls=%fused_computation.3.clone.1 | loop fusion | flops 5668864 | bytes 425472 | tf_op jit(solution)/shard_map/while/body/eval_jaxpr/reduce_sum | solution.py:126
  185.2 0.7 fusion.28
  185.9 0.7 copy-done.6
  186.6 1.0 fusion.24
  188.1 53.6 %all-reduce.4.cloned.1.call-done = (f32[256,256]{1,0:T(8,128)}, f32[256,256]{0,1:T(8,128)}) async-done(((f32[256,256]{1,0:T(8,128)}, f32[256,256]{0,1:T(8,128)}), (f32[256,256]{1,0:T(8,128)}, f32[256,256]{0,1:T(8,128)})) %all-reduce.4.cloned.1.call-update) | async-done | bytes 524304 | tf_op jit(solution)/shard_map/psum | solution.py:180
  241.7 1.4 fusion.23
  243.2 1.1 fusion.10
  244.4 0.8 copy-done.3
  245.1 15.0 %all_gather.15 = f32[1,2,256,256]{3,2,1,0:T(8,128)S(1)} all-gather(f32[1,2,32,256]{3,2,1,0:T(8,128)S(1)} %copy-done.3), channel_id=1, replica_groups=mesh['prow'=8,'pcol'=4] {'prow'}, dimensions={2}, use_global_device_ids=true | all-gather | bytes 589824 | tf_op jit(solution)/shard_map/all_gather | solution.py:167
  260.1 14.9 %all_gather.14 = f32[1,2,256,256]{3,2,1,0:T(8,128)S(1)} all-gather(f32[1,2,32,256]{3,2,1,0:T(8,128)S(1)} %copy-done.4), channel_id=1, replica_groups=mesh['prow'=8,'pcol'=4] {'prow'}, dimensions={2}, use_global_device_ids=true | all-gather | bytes 589824 | tf_op jit(solution)/shard_map/all_gather | solution.py:168
  276.6 1.3 fusion.60
  277.9 0.7 fusion.17
  278.6 0.7 fusion.21
  279.3 0.7 convolution_subtract_fusion
  280.0 0.7 convolution_add_fusion
  282.6 0.8 copy.55
  (218 shorter events, 11.1 us)
Async XLA Ops:
  6.5 235.2 %all-reduce.4.cloned.1.call-start = ((), (), s32[]{:S(2)}) async-start(), calls=%async_computation.1 | async-start | bytes 1048576 | tf_op jit(solution)/shard_map/psum | solution.py:180
  6.5 0.7 copy-start.8
  7.2 0.7 copy-start.9
  18.6 0.7 copy-start.7
  55.3 0.7 copy-start.5
  185.9 0.7 copy-start.6
  187.7 89.0 %all-gather.3.cloned.1.call-start = ((), (), s32[]{:S(2)}) async-start(), calls=%async_computation | async-start | bytes 1310720 | tf_op jit(solution)/shard_map/all_gather | solution.py:197
  241.7 1.4 copy-start.2
  244.3 0.8 copy-start.3
  245.1 15.0 %copy-start.4 = (f32[1,2,32,256]{3,2,1,0:T(8,128)S(1)}, f32[1,2,32,256]{3,2,1,0:T(8,128)}, u32[]{:S(2)}) copy-start(f32[1,2,32,256]{3,2,1,0:T(8,128)} %param.19) | copy-start | bytes 196612
  260.1 14.9 %copy-start.1 = (f32[256,256]{1,0:T(8,128)S(1)}, f32[256,256]{1,0:T(8,128)}, u32[]{:S(2)}) copy-start(f32[256,256]{1,0:T(8,128)} %get-tuple-element.613) | copy-start | bytes 786436
  281.0 1.0 copy-start
Sparse Core Ops, SparseCore 0:
  187.8 53.9 all-reduce.3
  244.4 25.5 all-gather.2
where the time goes:
time: 291 us; the launch traced here: 290 us
  other arithmetic  129 us (44%)
  blocking collectives  74.6 us (26%)
  waiting for transfers between devices  53.6 us (18%)
  between operations  14 us (5%)
  matrix products  9.77 us (3%)
  local copies, waits for them, and re-layouts  7.87 us (3%)
    reduce_sum x28, other arithmetic, one_point(): imag_sum = imag_sum + jnp.sum(factor * jnp.cos(phase_angle), axis=0)  125 us
    psum x1, waiting for transfers between devices, per_device(): incoming = lax.psum(incoming_part, 'prow')  53.6 us
    psum x2, blocking collectives, broadcast(): return lax.psum(block, axis)  36.6 us
    all_gather x1, blocking collectives, per_device(): lax.all_gather(lower_inv, 'prow', axis=2, tiled=True)  15 us
    all_gather x1, blocking collectives, per_device(): lax.all_gather(upper_inv, 'prow', axis=2, tiled=True)  14.9 us
    dot_general x19, matrix products, exact_dot(): return jnp.dot(first_matrix, second_matrix, precision=lax.Precision.HIGHEST)  9.77 us
    all_gather x1, blocking collectives, per_device(): row_block = lax.all_gather(tri_corners, 'pcol', axis=1, tiled=True)  8.18 us
  transfers between devices with their start and end apart: 2, of which 1 were waited for; matrix products, arithmetic and copies ran while one was open for 1% of the time, Pallas kernels for 0%

commit v1 on v0

--- a/solution.py
+++ b/solution.py
@@ -27,6 +27,14 @@
     0.125939180544827,
     0.125939180544827,
 )
+
+
+def sum_by_hops(array, axis):
+    n_dev, acc = (lax.axis_size(axis), array)
+    for hop in [1 << k for k in range(n_dev.bit_length() - 1)]:
+        swap = [(i, i ^ hop) for i in range(n_dev)]
+        acc = acc + lax.ppermute(acc, axis, swap)
+    return acc
 
 
 def broadcast(block, axis, owner):
@@ -177,7 +185,7 @@
     incoming_part = exact_dot(select, local_tile)
     local_start = 0 - owner_row * row_count
     diagonal_part = local_tile[local_start : local_start + PW]
-    incoming = lax.psum(incoming_part, "prow")
+    incoming = sum_by_hops(incoming_part, "prow")
     initial = broadcast(diagonal_part, "prow", owner_row)
     moved_rows = (
         (global_rows[:, None] == pivot_rows[None, :])

time: 291 us -> 294 us (1.010)
  waiting for transfers between devices: 53.6 us -> 58.1 us
    ppermute x0 -> x3, waiting for transfers between devices: none -> 9.35 us  [sum_by_hops(): acc = acc + lax.ppermute(acc, axis, swap)]
    psum x1, waiting for transfers between devices: 53.6 us -> 48.7 us  [broadcast(): return lax.psum(block, axis)]
  transfers between devices with their start and end apart: 2 -> 5, of which waited for: 1 -> 3; matrix products, arithmetic and copies ran while one was open for 1% -> 1% of each run, Pallas kernels for 0% -> 0%
where the time goes in v1:
time: 294 us
  other arithmetic  129 us (44%)
  blocking collectives  74.4 us (25%)
  waiting for transfers between devices  58.1 us (20%)
  between operations  14 us (5%)
  matrix products  9.03 us (3%)
  local copies, waits for them, and re-layouts  7.86 us (3%)
    reduce_sum x28, other arithmetic, one_point(): imag_sum = imag_sum + jnp.sum(factor * jnp.cos(phase_angle), axis=0)  125 us
    psum x1, waiting for transfers between devices, broadcast(): return lax.psum(block, axis)  48.7 us
    psum x2, blocking collectives, broadcast(): return lax.psum(block, axis)  36.6 us
    all_gather x1, blocking collectives, per_device(): lax.all_gather(lower_inv, 'prow', axis=2, tiled=True)  15 us
    all_gather x1, blocking collectives, per_device(): lax.all_gather(upper_inv, 'prow', axis=2, tiled=True)  14.7 us
    ppermute x3, waiting for transfers between devices, sum_by_hops(): acc = acc + lax.ppermute(acc, axis, swap)  9.35 us
    dot_general x19, matrix products, exact_dot(): return jnp.dot(first_matrix, second_matrix, precision=lax.Precision.HIGHEST)  9.03 us
    all_gather x1, blocking collectives, per_device(): row_block = lax.all_gather(tri_corners, 'pcol', axis=1, tiled=True)  8.18 us
  transfers between devices with their start and end apart: 5, of which 3 were waited for; matrix products, arithmetic and copies ran while one was open for 1% of the time, Pallas kernels for 0%

profile of v1, /device:TPU:0, one launch (start us, length us, event | category | flops | bytes accessed | tf_op | source)
XLA Modules:
  0.0 293.8 jit_solution(9061642003945568666)
XLA Ops:
  6.5 0.7 copy-done.6
  7.2 0.7 copy-done.7
  7.9 10.7 %psum.21 = s32[4,256]{1,0:T(4,128)S(1)} all-reduce(s32[4,256]{1,0:T(4,128)S(1)} %add_select_fusion), channel_id=1, replica_groups=mesh['prow'=8,'pcol'=4] {'prow'}, use_global_device_ids=true, to_apply=%region_6.8 | all-reduce | flops 1024 | bytes 8192 | tf_op jit(solution)/shard_map/psum | solution.py:42
  19.3 8.2 %all-gather = f32[4,64,9]{1,2,0:T(8,128)S(1)} all-gather(f32[1,64,9]{1,2,0:T(8,128)S(1)} %bitcast.272), channel_id=1, replica_groups=mesh['prow'=8,'pcol'=4] {'pcol'}, dimensions={0}, use_global_device_ids=true | all-gather | bytes 11520 | tf_op jit(solution)/shard_map/all_gather | solution.py:154
  27.9 25.9 %psum.22 = f32[9,256]{1,0:T(8,128)S(1)} all-reduce(f32[9,256]{1,0:T(8,128)S(1)} %select_bitcast_fusion), channel_id=1, replica_groups=mesh['prow'=8,'pcol'=4] {'prow'}, use_global_device_ids=true, to_apply=%region_5.7 | all-reduce | flops 2304 | bytes 18432 | tf_op jit(solution)/shard_map/psum | solution.py:42
  56.0 128.6 %while.18 = (s32[]{:T(128)}, f32[256,128]{1,0:T(8,128)S(1)}, f32[256,128]{1,0:T(8,128)S(1)}, f32[3,7,256]{2,1,0:T(8,128)S(1)}, f32[3,7,128]{2,1,0:T(8,128)S(1)},...) while((s32[]{:T(128)}, f32[256,128]{1,0:T(8,128)S(1)}, ...), condition=%wide.region_25.28_spmd.clone.clone.clone, body=%wide.region_16.27_spmd.clone.clone.clone.sunk | while | flops 23267076 | bytes 3925331 | solution.py:138
  56.4 4.5 %multiply_reduce_fusion.22 = (f32[256,128]{1,0:T(8,128)S(1)}, f32[256,128]{1,0:T(8,128)S(1)}) fusion(f32[256]{0:T(256)S(1)} %bitcast.245, f32[256]{0:T(256)S(1)} %bitcast.243, f32[256]{0:T(256)S(1)} %bitcast.241, f32[7,128]{1,0:T(8,128)S(1)} %get-tuple-element.877, f32[7,128]{1,0:T(8,128)S(1)} %get-tuple-element.878, ...), kind=kLoop, calls=%fused_computation.2.clone.1 | loop fusion | flops 5668864 | bytes 425472 | tf_op jit(solution)/shard_map/while/body/eval_jaxpr/reduce_sum | solution.py:134
  60.8 4.5 %multiply_reduce_fusion.24 = (f32[256,128]{1,0:T(8,128)S(1)}, f32[256,128]{1,0:T(8,128)S(1)}) fusion(f32[7,128]{1,0:T(8,128)S(1)} %get-tuple-element.877, f32[7,128]{1,0:T(8,128)S(1)} %get-tuple-element.878, f32[7,128]{1,0:T(8,128)S(1)} %get-tuple-element.879, f32[256]{0:T(256)S(1)} %bitcast.257, f32[256]{0:T(256)S(1)} %bitcast.255, ...), kind=kLoop, calls=%fused_computation.4.clone.1 | loop fusion | flops 5668864 | bytes 425472 | tf_op jit(solution)/shard_map/while/body/eval_jaxpr/reduce_sum | solution.py:134
  65.3 4.5 %multiply_reduce_fusion.25 = (f32[256,128]{1,0:T(8,128)S(1)}, f32[256,128]{1,0:T(8,128)S(1)}) fusion(f32[7,128]{1,0:T(8,128)S(1)} %get-tuple-element.889, f32[256]{0:T(256)S(1)} %bitcast.258, f32[7,128]{1,0:T(8,128)S(1)} %get-tuple-element.890, f32[256]{0:T(256)S(1)} %bitcast.256, f32[7,128]{1,0:T(8,128)S(1)} %get-tuple-element.891, ...), kind=kLoop, calls=%fused_computation.5.clone.1 | loop fusion | flops 5668864 | bytes 425472 | tf_op jit(solution)/shard_map/while/body/eval_jaxpr/reduce_sum | solution.py:134
  69.8 4.5 %multiply_reduce_fusion.23 = (f32[256,128]{1,0:T(8,128)S(1)}, f32[256,128]{1,0:T(8,128)S(1)}) fusion(f32[256]{0:T(256)S(1)} %bitcast.246, f32[256]{0:T(256)S(1)} %bitcast.244, f32[256]{0:T(256)S(1)} %bitcast.242, f32[7,128]{1,0:T(8,128)S(1)} %get-tuple-element.889, f32[7,128]{1,0:T(8,128)S(1)} %get-tuple-element.890, ...), kind=kLoop, calls=%fused_computation.3.clone.1 | loop fusion | flops 5668864 | bytes 425472 | tf_op jit(solution)/shard_map/while/body/eval_jaxpr/reduce_sum | solution.py:134
  74.7 4.5 %multiply_reduce_fusion.22 = (f32[256,128]{1,0:T(8,128)S(1)}, f32[256,128]{1,0:T(8,128)S(1)}) fusion(f32[256]{0:T(256)S(1)} %bitcast.245, f32[256]{0:T(256)S(1)} %bitcast.243, f32[256]{0:T(256)S(1)} %bitcast.241, f32[7,128]{1,0:T(8,128)S(1)} %get-tuple-element.877, f32[7,128]{1,0:T(8,128)S(1)} %get-tuple-element.878, ...), kind=kLoop, calls=%fused_computation.2.clone.1 | loop fusion | flops 5668864 | bytes 425472 | tf_op jit(solution)/shard_map/while/body/eval_jaxpr/reduce_sum | solution.py:134
  79.2 4.5 %multiply_reduce_fusion.24 = (f32[256,128]{1,0:T(8,128)S(1)}, f32[256,128]{1,0:T(8,128)S(1)}) fusion(f32[7,128]{1,0:T(8,128)S(1)} %get-tuple-element.877, f32[7,128]{1,0:T(8,128)S(1)} %get-tuple-element.878, f32[7,128]{1,0:T(8,128)S(1)} %get-tuple-element.879, f32[256]{0:T(256)S(1)} %bitcast.257, f32[256]{0:T(256)S(1)} %bitcast.255, ...), kind=kLoop, calls=%fused_computation.4.clone.1 | loop fusion | flops 5668864 | bytes 425472 | tf_op jit(solution)/shard_map/while/body/eval_jaxpr/reduce_sum | solution.py:134
  83.7 4.5 %multiply_reduce_fusion.25 = (f32[256,128]{1,0:T(8,128)S(1)}, f32[256,128]{1,0:T(8,128)S(1)}) fusion(f32[7,128]{1,0:T(8,128)S(1)} %get-tuple-element.889, f32[256]{0:T(256)S(1)} %bitcast.258, f32[7,128]{1,0:T(8,128)S(1)} %get-tuple-element.890, f32[256]{0:T(256)S(1)} %bitcast.256, f32[7,128]{1,0:T(8,128)S(1)} %get-tuple-element.891, ...), kind=kLoop, calls=%fused_computation.5.clone.1 | loop fusion | flops 5668864 | bytes 425472 | tf_op jit(solution)/shard_map/while/body/eval_jaxpr/reduce_sum | solution.py:134
  88.1 4.5 %multiply_reduce_fusion.23 = (f32[256,128]{1,0:T(8,128)S(1)}, f32[256,128]{1,0:T(8,128)S(1)}) fusion(f32[256]{0:T(256)S(1)} %bitcast.246, f32[256]{0:T(256)S(1)} %bitcast.244, f32[256]{0:T(256)S(1)} %bitcast.242, f32[7,128]{1,0:T(8,128)S(1)} %get-tuple-element.889, f32[7,128]{1,0:T(8,128)S(1)} %get-tuple-element.890, ...), kind=kLoop, calls=%fused_computation.3.clone.1 | loop fusion | flops 5668864 | bytes 425472 | tf_op jit(solution)/shard_map/while/body/eval_jaxpr/reduce_sum | solution.py:134
  93.1 4.5 %multiply_reduce_fusion.22 = (f32[256,128]{1,0:T(8,128)S(1)}, f32[256,128]{1,0:T(8,128)S(1)}) fusion(f32[256]{0:T(256)S(1)} %bitcast.245, f32[256]{0:T(256)S(1)} %bitcast.243, f32[256]{0:T(256)S(1)} %bitcast.241, f32[7,128]{1,0:T(8,128)S(1)} %get-tuple-element.877, f32[7,128]{1,0:T(8,128)S(1)} %get-tuple-element.878, ...), kind=kLoop, calls=%fused_computation.2.clone.1 | loop fusion | flops 5668864 | bytes 425472 | tf_op jit(solution)/shard_map/while/body/eval_jaxpr/reduce_sum | solution.py:134
  97.6 4.5 %multiply_reduce_fusion.24 = (f32[256,128]{1,0:T(8,128)S(1)}, f32[256,128]{1,0:T(8,128)S(1)}) fusion(f32[7,128]{1,0:T(8,128)S(1)} %get-tuple-element.877, f32[7,128]{1,0:T(8,128)S(1)} %get-tuple-element.878, f32[7,128]{1,0:T(8,128)S(1)} %get-tuple-element.879, f32[256]{0:T(256)S(1)} %bitcast.257, f32[256]{0:T(256)S(1)} %bitcast.255, ...), kind=kLoop, calls=%fused_computation.4.clone.1 | loop fusion | flops 5668864 | bytes 425472 | tf_op jit(solution)/shard_map/while/body/eval_jaxpr/reduce_sum | solution.py:134
  102.0 4.5 %multiply_reduce_fusion.25 = (f32[256,128]{1,0:T(8,128)S(1)}, f32[256,128]{1,0:T(8,128)S(1)}) fusion(f32[7,128]{1,0:T(8,128)S(1)} %get-tuple-element.889, f32[256]{0:T(256)S(1)} %bitcast.258, f32[7,128]{1,0:T(8,128)S(1)} %get-tuple-element.890, f32[256]{0:T(256)S(1)} %bitcast.256, f32[7,128]{1,0:T(8,128)S(1)} %get-tuple-element.891, ...), kind=kLoop, calls=%fused_computation.5.clone.1 | loop fusion | flops 5668864 | bytes 425472 | tf_op jit(solution)/shard_map/while/body/eval_jaxpr/reduce_sum | solution.py:134
  106.5 4.5 %multiply_reduce_fusion.23 = (f32[256,128]{1,0:T(8,128)S(1)}, f32[256,128]{1,0:T(8,128)S(1)}) fusion(f32[256]{0:T(256)S(1)} %bitcast.246, f32[256]{0:T(256)S(1)} %bitcast.244, f32[256]{0:T(256)S(1)} %bitcast.242, f32[7,128]{1,0:T(8,128)S(1)} %get-tuple-element.889, f32[7,128]{1,0:T(8,128)S(1)} %get-tuple-element.890, ...), kind=kLoop, calls=%fused_computation.3.clone.1 | loop fusion | flops 5668864 | bytes 425472 | tf_op jit(solution)/shard_map/while/body/eval_jaxpr/reduce_sum | solution.py:134
  111.5 4.5 %multiply_reduce_fusion.22 = (f32[256,128]{1,0:T(8,128)S(1)}, f32[256,128]{1,0:T(8,128)S(1)}) fusion(f32[256]{0:T(256)S(1)} %bitcast.245, f32[256]{0:T(256)S(1)} %bitcast.243, f32[256]{0:T(256)S(1)} %bitcast.241, f32[7,128]{1,0:T(8,128)S(1)} %get-tuple-element.877, f32[7,128]{1,0:T(8,128)S(1)} %get-tuple-element.878, ...), kind=kLoop, calls=%fused_computation.2.clone.1 | loop fusion | flops 5668864 | bytes 425472 | tf_op jit(solution)/shard_map/while/body/eval_jaxpr/reduce_sum | solution.py:134
  115.9 4.5 %multiply_reduce_fusion.24 = (f32[256,128]{1,0:T(8,128)S(1)}, f32[256,128]{1,0:T(8,128)S(1)}) fusion(f32[7,128]{1,0:T(8,128)S(1)} %get-tuple-element.877, f32[7,128]{1,0:T(8,128)S(1)} %get-tuple-element.878, f32[7,128]{1,0:T(8,128)S(1)} %get-tuple-element.879, f32[256]{0:T(256)S(1)} %bitcast.257, f32[256]{0:T(256)S(1)} %bitcast.255, ...), kind=kLoop, calls=%fused_computation.4.clone.1 | loop fusion | flops 5668864 | bytes 425472 | tf_op jit(solution)/shard_map/while/body/eval_jaxpr/reduce_sum | solution.py:134
  120.4 4.5 %multiply_reduce_fusion.25 = (f32[256,128]{1,0:T(8,128)S(1)}, f32[256,128]{1,0:T(8,128)S(1)}) fusion(f32[7,128]{1,0:T(8,128)S(1)} %get-tuple-element.889, f32[256]{0:T(256)S(1)} %bitcast.258, f32[7,128]{1,0:T(8,128)S(1)} %get-tuple-element.890, f32[256]{0:T(256)S(1)} %bitcast.256, f32[7,128]{1,0:T(8,128)S(1)} %get-tuple-element.891, ...), kind=kLoop, calls=%fused_computation.5.clone.1 | loop fusion | flops 5668864 | bytes 425472 | tf_op jit(solution)/shard_map/while/body/eval_jaxpr/reduce_sum | solution.py:134
  124.9 4.5 %multiply_reduce_fusion.23 = (f32[256,128]{1,0:T(8,128)S(1)}, f32[256,128]{1,0:T(8,128)S(1)}) fusion(f32[256]{0:T(256)S(1)} %bitcast.246, f32[256]{0:T(256)S(1)} %bitcast.244, f32[256]{0:T(256)S(1)} %bitcast.242, f32[7,128]{1,0:T(8,128)S(1)} %get-tuple-element.889, f32[7,128]{1,0:T(8,128)S(1)} %get-tuple-element.890, ...), kind=kLoop, calls=%fused_computation.3.clone.1 | loop fusion | flops 5668864 | bytes 425472 | tf_op jit(solution)/shard_map/while/body/eval_jaxpr/reduce_sum | solution.py:134
  129.9 4.5 %multiply_reduce_fusion.22 = (f32[256,128]{1,0:T(8,128)S(1)}, f32[256,128]{1,0:T(8,128)S(1)}) fusion(f32[256]{0:T(256)S(1)} %bitcast.245, f32[256]{0:T(256)S(1)} %bitcast.243, f32[256]{0:T(256)S(1)} %bitcast.241, f32[7,128]{1,0:T(8,128)S(1)} %get-tuple-element.877, f32[7,128]{1,0:T(8,128)S(1)} %get-tuple-element.878, ...), kind=kLoop, calls=%fused_computation.2.clone.1 | loop fusion | flops 5668864 | bytes 425472 | tf_op jit(solution)/shard_map/while/body/eval_jaxpr/reduce_sum | solution.py:134
  134.3 4.5 %multiply_reduce_fusion.24 = (f32[256,128]{1,0:T(8,128)S(1)}, f32[256,128]{1,0:T(8,128)S(1)}) fusion(f32[7,128]{1,0:T(8,128)S(1)} %get-tuple-element.877, f32[7,128]{1,0:T(8,128)S(1)} %get-tuple-element.878, f32[7,128]{1,0:T(8,128)S(1)} %get-tuple-element.879, f32[256]{0:T(256)S(1)} %bitcast.257, f32[256]{0:T(256)S(1)} %bitcast.255, ...), kind=kLoop, calls=%fused_computation.4.clone.1 | loop fusion | flops 5668864 | bytes 425472 | tf_op jit(solution)/shard_map/while/body/eval_jaxpr/reduce_sum | solution.py:134
  138.8 4.5 %multiply_reduce_fusion.25 = (f32[256,128]{1,0:T(8,128)S(1)}, f32[256,128]{1,0:T(8,128)S(1)}) fusion(f32[7,128]{1,0:T(8,128)S(1)} %get-tuple-element.889, f32[256]{0:T(256)S(1)} %bitcast.258, f32[7,128]{1,0:T(8,128)S(1)} %get-tuple-element.890, f32[256]{0:T(256)S(1)} %bitcast.256, f32[7,128]{1,0:T(8,128)S(1)} %get-tuple-element.891, ...), kind=kLoop, calls=%fused_computation.5.clone.1 | loop fusion | flops 5668864 | bytes 425472 | tf_op jit(solution)/shard_map/while/body/eval_jaxpr/reduce_sum | solution.py:134
  143.2 4.5 %multiply_reduce_fusion.23 = (f32[256,128]{1,0:T(8,128)S(1)}, f32[256,128]{1,0:T(8,128)S(1)}) fusion(f32[256]{0:T(256)S(1)} %bitcast.246, f32[256]{0:T(256)S(1)} %bitcast.244, f32[256]{0:T(256)S(1)} %bitcast.242, f32[7,128]{1,0:T(8,128)S(1)} %get-tuple-element.889, f32[7,128]{1,0:T(8,128)S(1)} %get-tuple-element.890, ...), kind=kLoop, calls=%fused_computation.3.clone.1 | loop fusion | flops 5668864 | bytes 425472 | tf_op jit(solution)/shard_map/while/body/eval_jaxpr/reduce_sum | solution.py:134
  148.2 4.5 %multiply_reduce_fusion.22 = (f32[256,128]{1,0:T(8,128)S(1)}, f32[256,128]{1,0:T(8,128)S(1)}) fusion(f32[256]{0:T(256)S(1)} %bitcast.245, f32[256]{0:T(256)S(1)} %bitcast.243, f32[256]{0:T(256)S(1)} %bitcast.241, f32[7,128]{1,0:T(8,128)S(1)} %get-tuple-element.877, f32[7,128]{1,0:T(8,128)S(1)} %get-tuple-element.878, ...), kind=kLoop, calls=%fused_computation.2.clone.1 | loop fusion | flops 5668864 | bytes 425472 | tf_op jit(solution)/shard_map/while/body/eval_jaxpr/reduce_sum | solution.py:134
  152.7 4.5 %multiply_reduce_fusion.24 = (f32[256,128]{1,0:T(8,128)S(1)}, f32[256,128]{1,0:T(8,128)S(1)}) fusion(f32[7,128]{1,0:T(8,128)S(1)} %get-tuple-element.877, f32[7,128]{1,0:T(8,128)S(1)} %get-tuple-element.878, f32[7,128]{1,0:T(8,128)S(1)} %get-tuple-element.879, f32[256]{0:T(256)S(1)} %bitcast.257, f32[256]{0:T(256)S(1)} %bitcast.255, ...), kind=kLoop, calls=%fused_computation.4.clone.1 | loop fusion | flops 5668864 | bytes 425472 | tf_op jit(solution)/shard_map/while/body/eval_jaxpr/reduce_sum | solution.py:134
  157.2 4.5 %multiply_reduce_fusion.25 = (f32[256,128]{1,0:T(8,128)S(1)}, f32[256,128]{1,0:T(8,128)S(1)}) fusion(f32[7,128]{1,0:T(8,128)S(1)} %get-tuple-element.889, f32[256]{0:T(256)S(1)} %bitcast.258, f32[7,128]{1,0:T(8,128)S(1)} %get-tuple-element.890, f32[256]{0:T(256)S(1)} %bitcast.256, f32[7,128]{1,0:T(8,128)S(1)} %get-tuple-element.891, ...), kind=kLoop, calls=%fused_computation.5.clone.1 | loop fusion | flops 5668864 | bytes 425472 | tf_op jit(solution)/shard_map/while/body/eval_jaxpr/reduce_sum | solution.py:134
  161.6 4.5 %multiply_reduce_fusion.23 = (f32[256,128]{1,0:T(8,128)S(1)}, f32[256,128]{1,0:T(8,128)S(1)}) fusion(f32[256]{0:T(256)S(1)} %bitcast.246, f32[256]{0:T(256)S(1)} %bitcast.244, f32[256]{0:T(256)S(1)} %bitcast.242, f32[7,128]{1,0:T(8,128)S(1)} %get-tuple-element.889, f32[7,128]{1,0:T(8,128)S(1)} %get-tuple-element.890, ...), kind=kLoop, calls=%fused_computation.3.clone.1 | loop fusion | flops 5668864 | bytes 425472 | tf_op jit(solution)/shard_map/while/body/eval_jaxpr/reduce_sum | solution.py:134
  166.6 4.5 %multiply_reduce_fusion.22 = (f32[256,128]{1,0:T(8,128)S(1)}, f32[256,128]{1,0:T(8,128)S(1)}) fusion(f32[256]{0:T(256)S(1)} %bitcast.245, f32[256]{0:T(256)S(1)} %bitcast.243, f32[256]{0:T(256)S(1)} %bitcast.241, f32[7,128]{1,0:T(8,128)S(1)} %get-tuple-element.877, f32[7,128]{1,0:T(8,128)S(1)} %get-tuple-element.878, ...), kind=kLoop, calls=%fused_computation.2.clone.1 | loop fusion | flops 5668864 | bytes 425472 | tf_op jit(solution)/shard_map/while/body/eval_jaxpr/reduce_sum | solution.py:134
  171.1 4.5 %multiply_reduce_fusion.24 = (f32[256,128]{1,0:T(8,128)S(1)}, f32[256,128]{1,0:T(8,128)S(1)}) fusion(f32[7,128]{1,0:T(8,128)S(1)} %get-tuple-element.877, f32[7,128]{1,0:T(8,128)S(1)} %get-tuple-element.878, f32[7,128]{1,0:T(8,128)S(1)} %get-tuple-element.879, f32[256]{0:T(256)S(1)} %bitcast.257, f32[256]{0:T(256)S(1)} %bitcast.255, ...), kind=kLoop, calls=%fused_computation.4.clone.1 | loop fusion | flops 5668864 | bytes 425472 | tf_op jit(solution)/shard_map/while/body/eval_jaxpr/reduce_sum | solution.py:134
  175.5 4.5 %multiply_reduce_fusion.25 = (f32[256,128]{1,0:T(8,128)S(1)}, f32[256,128]{1,0:T(8,128)S(1)}) fusion(f32[7,128]{1,0:T(8,128)S(1)} %get-tuple-element.889, f32[256]{0:T(256)S(1)} %bitcast.258, f32[7,128]{1,0:T(8,128)S(1)} %get-tuple-element.890, f32[256]{0:T(256)S(1)} %bitcast.256, f32[7,128]{1,0:T(8,128)S(1)} %get-tuple-element.891, ...), kind=kLoop, calls=%fused_computation.5.clone.1 | loop fusion | flops 5668864 | bytes 425472 | tf_op jit(solution)/shard_map/while/body/eval_jaxpr/reduce_sum | solution.py:134
  180.0 4.5 %multiply_reduce_fusion.23 = (f32[256,128]{1,0:T(8,128)S(1)}, f32[256,128]{1,0:T(8,128)S(1)}) fusion(f32[256]{0:T(256)S(1)} %bitcast.246, f32[256]{0:T(256)S(1)} %bitcast.244, f32[256]{0:T(256)S(1)} %bitcast.242, f32[7,128]{1,0:T(8,128)S(1)} %get-tuple-element.889, f32[7,128]{1,0:T(8,128)S(1)} %get-tuple-element.890, ...), kind=kLoop, calls=%fused_computation.3.clone.1 | loop fusion | flops 5668864 | bytes 425472 | tf_op jit(solution)/shard_map/while/body/eval_jaxpr/reduce_sum | solution.py:134
  185.9 0.7 fusion.26
  187.8 8.8 %collective-permute-done.1 = f32[256,256]{1,0:T(8,128)S(1)} collective-permute-done((f32[256,256]{1,0:T(8,128)S(1)}, f32[256,256]{1,0:T(8,128)S(1)}, u32[]{:S(2)}, u32[]{:S(2)}) %collective-permute-start.1) | collective-permute-done | bytes 262176 | tf_op jit(solution)/shard_map/ppermute | solution.py:36
  196.7 48.7 %all-reduce.3.cloned.1.call-done = f32[256,256]{0,1:T(8,128)} async-done(((f32[256,256]{0,1:T(8,128)}), f32[256,256]{0,1:T(8,128)}) %all-reduce.3.cloned.1.call-update) | async-done | bytes 262160 | tf_op jit(solution)/shard_map/psum | solution.py:42
  245.4 1.4 convolution_select_fusion
  246.8 1.1 convolution_select_fusion.1
  248.0 0.8 copy-done.1
  248.8 15.0 %all_gather.15 = f32[1,2,256,256]{3,2,1,0:T(8,128)S(1)} all-gather(f32[1,2,32,256]{3,2,1,0:T(8,128)S(1)} %copy-done.1), channel_id=1, replica_groups=mesh['prow'=8,'pcol'=4] {'prow'}, dimensions={2}, use_global_device_ids=true | all-gather | bytes 589824 | tf_op jit(solution)/shard_map/all_gather | solution.py:175
  263.7 14.7 %all_gather.14 = f32[1,2,256,256]{3,2,1,0:T(8,128)S(1)} all-gather(f32[1,2,32,256]{3,2,1,0:T(8,128)S(1)} %copy-done.2), channel_id=1, replica_groups=mesh['prow'=8,'pcol'=4] {'prow'}, dimensions={2}, use_global_device_ids=true | all-gather | bytes 589824 | tf_op jit(solution)/shard_map/all_gather | solution.py:176
  280.1 1.3 fusion.58
  281.4 0.7 fusion.16
  282.1 0.7 fusion.20
  282.8 0.7 convolution_subtract_fusion
  283.5 0.7 convolution_add_fusion
  286.1 0.8 copy.55
  (223 shorter events, 12.0 us)
Async XLA Ops:
  6.5 238.8 %all-reduce.3.cloned.1.call-start = ((), (), s32[]{:S(2)}) async-start(), calls=%async_computation | async-start | bytes 524288 | tf_op jit(solution)/shard_map/psum | solution.py:42
  6.5 0.7 copy-start.6
  7.2 0.7 copy-start.7
  18.6 0.7 copy-start.5
  55.3 0.7 copy-start.3
  184.8 0.7 copy-start.4
  185.8 1.6 collective-permute-start
  186.7 93.4 %all-gather.3.cloned.1.call-start = ((), (), s32[]{:S(2)}) async-start(), calls=%async_computation.1 | async-start | bytes 1310720 | tf_op jit(solution)/shard_map/all_gather | solution.py:205
  187.5 9.1 %collective-permute-start.1 = (f32[256,256]{1,0:T(8,128)S(1)}, f32[256,256]{1,0:T(8,128)S(1)}, u32[]{:S(2)}, u32[]{:S(2)}) collective-permute-start(f32[256,256]{1,0:T(8,128)S(1)} %add.524), channel_id=1, source_target_pairs={{0,8},{4,12},{8,0},{12,4},{16,24},{20,28},{24,16},{28,20},{1,9},{5... | collective-permute-start | bytes 786440 | tf_op jit(solution)/shard_map/ppermute | solution.py:36
  196.6 50.1 %collective-permute-start.2 = (f32[256,256]{1,0:T(8,128)S(1)}, f32[256,256]{1,0:T(8,128)S(1)}, u32[]{:S(2)}, u32[]{:S(2)}) collective-permute-start(f32[256,256]{1,0:T(8,128)S(1)} %add.525), channel_id=1, source_target_pairs={{0,16},{4,20},{8,24},{12,28},{16,0},{20,4},{24,8},{28,12},{1,17},{... | collective-permute-start | bytes 786440 | tf_op jit(solution)/shard_map/ppermute | solution.py:36
  247.9 0.8 copy-start.1
  248.8 15.0 %copy-start.2 = (f32[1,2,32,256]{3,2,1,0:T(8,128)S(1)}, f32[1,2,32,256]{3,2,1,0:T(8,128)}, u32[]{:S(2)}) copy-start(f32[1,2,32,256]{3,2,1,0:T(8,128)} %param.19) | copy-start | bytes 196612
  284.5 1.0 copy-start
Sparse Core Ops, SparseCore 0:
  186.8 58.5 all-reduce.2
  248.1 25.5 all-gather.2
